TPU v7x, 32 devices: a whole 2x2x4 slice. The times are simulated.
32 devices in a mesh: grp: 4 (over x, core), mem: 8 (over z, y).
Axes of the slice: x: 2, y: 2, z: 4, core: 2. Of those that a mesh axis runs over, the one named last changes fastest.
Arguments:
- leaf_fronts: float32 [4, 4096, 4096], P('grp', None, 'mem'), as said below
- block_owner: int32 [4, 32], P('grp', 'mem'), may hold values from 0 to 31, as said below
- root_front: float32 [4096, 4096], P('grp', 'mem'), as said below
Outputs:
- root_factor: float32 [4096, 4096], P('grp', 'mem')
- log_det: float32 [5], replicated
Inputs may be any that keep to these rules, and one draw needn't show every extreme that they name: Each row of block_owner is a permutation of 0 to 31. For each g, the matrix whose column block block_owner[g, t] is column block t of leaf_fronts[g] is symmetric positive definite. root_front is symmetric positive definite.
All inputs are finite; a program needn't handle non-finite values.
Results may differ from a plain program's by a relative error of at most 0.0021.
Values may be sent and summed in bfloat16 or wider, within the bound.
No kernel may reach another device: no remote copies, remote signals or barrier semaphores. Data moves between devices by JAX's collectives and lax.ppermute only.
A program may use at most 64 MiB of HBM per device.

v0:
```python
import jax
import jax.numpy as jnp
from jax import lax
from jax.sharding import PartitionSpec as P

PL = 3
PR = 2


def broadcast(value, axis, root):
    mine = lax.axis_index(axis) == root
    return lax.psum(jnp.where(mine, value, jnp.zeros_like(value)), axis)


def factor_panel(column, diagonal_block, holder, first_row, row_ids):
    eye_block = jnp.eye(diagonal_block.shape[0], dtype=jnp.float32)
    factor = jnp.linalg.cholesky(jnp.where(holder, diagonal_block, eye_block))
    panel_rows = lax.linalg.triangular_solve(
        factor, column, left_side=False, lower=True, transpose_a=True
    )
    panel_rows = jnp.where((row_ids >= first_row)[:, None], panel_rows, jnp.zeros_like(panel_rows))
    log_sum = 2.0 * jnp.sum(jnp.log(jnp.diagonal(factor)))
    return (panel_rows, log_sum)


def local(leaf_fronts, block_owner, root_front):
    members = lax.axis_size("mem")
    groups = lax.axis_size("grp")
    member = lax.axis_index("mem")
    my_group = lax.axis_index("grp")
    leaf_local = leaf_fronts[0]
    front_order = leaf_local.shape[0]
    owner_local = block_owner[0]
    per_member = owner_local.shape[0]
    block_width = front_order // (per_member * members)
    block_count = front_order // block_width
    cols_local = per_member * block_width
    owner_full = lax.all_gather(block_owner, "mem", axis=1, tiled=True)[0]
    slot_ids = jnp.arange(block_count, dtype=jnp.int32)
    row_ids = jnp.arange(front_order, dtype=jnp.int32)
    blocks = leaf_local.reshape(front_order, per_member, block_width)
    leaf_logs = jnp.zeros((), jnp.float32)
    for section_index in range(PL):
        holds_block = owner_local == section_index
        holder = jnp.any(holds_block)
        column = jnp.sum(jnp.where(holds_block[None, :, None], blocks, 0.0), axis=1)
        diagonal_block = column[section_index * block_width : (section_index + 1) * block_width]
        panel_rows, log_sum = factor_panel(
            column, diagonal_block, holder, section_index * block_width, row_ids
        )
        leaf_logs = leaf_logs + jnp.where(holder, log_sum, 0.0)
        source = jnp.sum(jnp.where(owner_full == section_index, slot_ids, 0)) // per_member
        shared = broadcast(panel_rows.astype(jnp.bfloat16), "mem", source)
        across = jnp.take(
            shared.reshape(block_count, block_width, block_width), owner_local, axis=0
        )
        blocks = blocks - jnp.einsum(
            "rc,jbc->rjb", shared, across, preferred_element_type=jnp.float32
        )
    keep_cols = owner_local >= PL
    masked = jnp.where(keep_cols[None, :, None], blocks, 0.0).reshape(
        block_count, block_width, cols_local
    )
    quarter_rows = root_front.shape[0]
    root_logs = jnp.zeros((), jnp.float32)
    placed_front = lax.dynamic_update_slice_in_dim(
        jnp.zeros((front_order, cols_local), jnp.float32), root_front, my_group * quarter_rows, 0
    )
    taken = jnp.take(masked, owner_full, axis=0)
    placed = jnp.where((owner_full >= PL)[:, None, None], taken, 0.0)
    root_full = lax.psum(placed.reshape(front_order, cols_local) + placed_front, "grp")
    panels_full = jnp.zeros_like(root_full)
    for section_index in range(PR):
        owner_member, local_slot = divmod(section_index, per_member)
        column = root_full[:, local_slot * block_width : (local_slot + 1) * block_width]
        diagonal_block = column[section_index * block_width : (section_index + 1) * block_width]
        holder = member == owner_member
        panel_rows, log_sum = factor_panel(
            column, diagonal_block, holder, section_index * block_width, row_ids
        )
        root_logs = root_logs + jnp.where(holder & (my_group == 0), log_sum, 0.0)
        full_panel = broadcast(panel_rows.astype(jnp.bfloat16), "mem", owner_member)
        col_rows = lax.dynamic_slice_in_dim(full_panel, member * cols_local, cols_local, 0)
        root_full = root_full - jnp.einsum(
            "rc,xc->rx", full_panel, col_rows, preferred_element_type=jnp.float32
        )
        kept_block = panels_full[:, local_slot * block_width : (local_slot + 1) * block_width]
        panels_full = panels_full.at[
            :, local_slot * block_width : (local_slot + 1) * block_width
        ].set(jnp.where(holder, panel_rows, kept_block))
    root_local = lax.dynamic_slice_in_dim(root_full, my_group * quarter_rows, quarter_rows, 0)
    panels_kept = lax.dynamic_slice_in_dim(panels_full, my_group * quarter_rows, quarter_rows, 0)
    global_rows = my_group * quarter_rows + jnp.arange(quarter_rows, dtype=jnp.int32)
    column_blocks = member * per_member + jnp.arange(per_member, dtype=jnp.int32)
    pivot_cols = jnp.repeat(column_blocks < PR, block_width, total_repeat_length=cols_local)
    trailing = jnp.where((global_rows >= PR * block_width)[:, None], root_local, 0.0)
    root_factor = jnp.where(pivot_cols[None, :], panels_kept, trailing)
    places = jnp.arange(groups + 1, dtype=jnp.int32)
    terms = jnp.where(places == my_group, leaf_logs / (PL * block_width), 0.0) + jnp.where(
        places == groups, root_logs / (PR * block_width), 0.0
    )
    log_det = lax.psum(terms, ("grp", "mem"))
    return (root_factor, log_det)


def solution(mesh):
    in_specs = (P("grp", None, "mem"), P("grp", "mem"), P("grp", "mem"))
    out_specs = (P("grp", "mem"), P())
    return jax.shard_map(local, mesh=mesh, in_specs=in_specs, out_specs=out_specs, check_vma=False)
```

profile of v0, /device:TPU:0, one launch (start us, length us, event | category | flops | bytes accessed | tf_op | source)
XLA Modules:
  0.0 842.2 jit_solution(10672149471551786729)
XLA Ops:
  9.9 13.1 %all-reduce.1 = s32[32]{0:T(128)S(1)} all-reduce(s32[32]{0:T(128)S(1)} %get-tuple-element.74), channel_id=1, replica_groups=mesh['grp'=4,'mem'=8] {'mem'}, use_global_device_ids=true, to_apply=%add.1 | all-reduce | flops 32 | bytes 256 | tf_op jit(solution)/shard_map/squeeze | solution.py:38
  27.6 8.9 %copy.38 = f32[1,4096,512]{1,2,0:T(8,128)} copy(f32[1,4096,512]{2,1,0:T(8,128)} %param.14) | data formatting | bytes 16777216 | tf_op args[0]
  36.6 8.9 %copy.44 = f32[4096,4,128]{2,0,1:T(8,128)} copy(f32[4096,4,128]{0,2,1:T(8,128)} %bitcast.141) | data formatting | bytes 16777216 | tf_op jit(solution)/shard_map/reshape;squeeze | solution.py:41
  51.4 11.7 %cholesky.89 = f32[128,128]{1,0:T(8,128)S(1)} custom-call(f32[128,128]{1,0:T(8,128)S(1)} %fusion.34), custom_call_target="Cholesky" | custom-call | tf_op jit(solution)/shard_map/jit(cholesky)/cholesky | solution.py:17
  64.4 9.8 %custom-call.19 = f32[1,128,128]{1,2,0:T(8,128)S(1)} custom-call(f32[1,128,128]{2,1,0:T(8,128)S(1)} %get-tuple-element.61), custom_call_target="InvertDiagBlocksLowerTriangular" | custom-call | tf_op jit(solution)/shard_map/triangular_solve/custom-call.0 | solution.py:18
  79.8 73.8 %all-reduce.9.cloned.1.call-done = bf16[4096,128]{0,1:T(8,128)(2,1)} async-done(((bf16[4096,128]{0,1:T(8,128)(2,1)}), bf16[4096,128]{0,1:T(8,128)(2,1)}) %all-reduce.9.cloned.1.call-update) | async-done | bytes 1048592 | tf_op jit(solution)/shard_map/psum | solution.py:12
  155.8 8.8 %select_reduce_fusion.1 = (f32[4096,128]{1,0:T(8,128)S(1)}, f32[4096,4,128]{2,0,1:T(8,128)}) fusion(pred[4]{0:T(512)(128)(4,1)S(1)} %get-tuple-element.71, f32[4096,4,128]{2,0,1:T(8,128)} %copy.44, bf16[4,128,128]{2,1,0:T(8,128)(2,1)S(1)} %gather_fusion.6, pred[4]{0:T(512)(128)(4,1)S(1)} %get-tuple-element.72, ...), kind=kOutput, calls=%fused_computation.12 | convolution fusion | flops 542703616 | bytes 20054024 | tf_op jit(solution)/shard_map/rc,jbc->rjb/dot_general | solution.py:57
  166.0 11.7 %cholesky.100 = f32[128,128]{1,0:T(8,128)S(1)} custom-call(f32[128,128]{1,0:T(8,128)S(1)} %fusion.32), custom_call_target="Cholesky" | custom-call | tf_op jit(solution)/shard_map/jit(cholesky)/cholesky | solution.py:17
  179.0 9.8 %custom-call.20 = f32[1,128,128]{1,2,0:T(8,128)S(1)} custom-call(f32[1,128,128]{2,1,0:T(8,128)S(1)} %get-tuple-element.59), custom_call_target="InvertDiagBlocksLowerTriangular" | custom-call | tf_op jit(solution)/shard_map/triangular_solve/custom-call.0 | solution.py:18
  194.8 74.7 %all-reduce.11.cloned.1.call-done = bf16[4096,128]{0,1:T(8,128)(2,1)} async-done(((bf16[4096,128]{0,1:T(8,128)(2,1)}), bf16[4096,128]{0,1:T(8,128)(2,1)}) %all-reduce.11.cloned.1.call-update) | async-done | bytes 1048592 | tf_op jit(solution)/shard_map/psum | solution.py:12
  271.7 8.8 %select_reduce_fusion = (f32[4096,128]{1,0:T(8,128)S(1)}, f32[4096,4,128]{2,0,1:T(8,128)}) fusion(pred[4]{0:T(512)(128)(4,1)S(1)} %get-tuple-element.69, f32[4096,4,128]{2,0,1:T(8,128)} %get-tuple-element.77, bf16[4,128,128]{2,1,0:T(8,128)(2,1)S(1)} %gather_fusion.7, pred[4]{0:T(512)(128)(4,1)S(1)} %get-tuple-element.72, ...), kind=kOutput, calls=%fused_computation.11 | convolution fusion | flops 542703616 | bytes 20054024 | tf_op jit(solution)/shard_map/rc,jbc->rjb/dot_general | solution.py:57
  282.1 11.7 %cholesky.111 = f32[128,128]{1,0:T(8,128)S(1)} custom-call(f32[128,128]{1,0:T(8,128)S(1)} %fusion.30), custom_call_target="Cholesky" | custom-call | tf_op jit(solution)/shard_map/jit(cholesky)/cholesky | solution.py:17
  295.1 9.8 %custom-call.21 = f32[1,128,128]{1,2,0:T(8,128)S(1)} custom-call(f32[1,128,128]{2,1,0:T(8,128)S(1)} %get-tuple-element.57), custom_call_target="InvertDiagBlocksLowerTriangular" | custom-call | tf_op jit(solution)/shard_map/triangular_solve/custom-call.0 | solution.py:18
  310.2 75.5 %all-reduce.13.cloned.1.call-done = bf16[4096,128]{0,1:T(8,128)(2,1)} async-done(((bf16[4096,128]{0,1:T(8,128)(2,1)}), bf16[4096,128]{0,1:T(8,128)(2,1)}) %all-reduce.13.cloned.1.call-update) | async-done | bytes 1048592 | tf_op jit(solution)/shard_map/psum | solution.py:12
  387.9 5.5 subtract_select_fusion
  393.5 18.6 %copy.73 = f32[4096,4,128]{2,1,0:T(4,128)} copy(f32[4096,4,128]{2,0,1:T(8,128)S(1)} %subtract_select_fusion) | data formatting | bytes 16777216 | tf_op jit(solution)/shard_map/reshape | solution.py:61
  412.1 10.3 %reshape.387 = f32[32,128,512]{2,1,0:T(8,128)} reshape(f32[4096,4,128]{2,1,0:T(4,128)} %copy.73) | data formatting | bytes 16777216 | tf_op jit(solution)/shard_map/reshape | solution.py:61
  422.4 7.7 gather_fusion
  430.1 8.9 %copy.74 = f32[4096,512]{0,1:T(8,128)} copy(f32[4096,512]{1,0:T(8,128)} %bitcast.140) | data formatting | bytes 16777216 | tf_op jit(solution)/shard_map/jit(_take)/gather | solution.py:69
  439.0 8.3 select_select_fusion
  465.0 138.2 %all-reduce.15.cloned.1.call-done = f32[4096,512]{0,1:T(8,128)} async-done(((f32[4096,512]{0,1:T(8,128)}), f32[4096,512]{0,1:T(8,128)}) %all-reduce.15.cloned.1.call-update) | async-done | bytes 8388624 | tf_op jit(solution)/shard_map/psum | solution.py:71
  605.0 11.7 %cholesky.122 = f32[128,128]{1,0:T(8,128)S(1)} custom-call(f32[128,128]{1,0:T(8,128)S(1)} %fusion.28), custom_call_target="Cholesky" | custom-call | tf_op jit(solution)/shard_map/jit(cholesky)/cholesky | solution.py:17
  618.0 9.8 %custom-call.22 = f32[1,128,128]{1,2,0:T(8,128)S(1)} custom-call(f32[1,128,128]{2,1,0:T(8,128)S(1)} %get-tuple-element.55), custom_call_target="InvertDiagBlocksLowerTriangular" | custom-call | tf_op jit(solution)/shard_map/triangular_solve/custom-call.0 | solution.py:18
  627.8 4.5 convert_select_fusion.1
  637.4 73.4 %all-reduce.17.cloned.1.call-done = bf16[4096,128]{0,1:T(8,128)(2,1)} async-done(((bf16[4096,128]{0,1:T(8,128)(2,1)}), bf16[4096,128]{0,1:T(8,128)(2,1)}) %all-reduce.17.cloned.1.call-update) | async-done | bytes 1048592 | tf_op jit(solution)/shard_map/psum | solution.py:12
  710.8 5.1 convolution_subtract_fusion
  720.1 11.7 %cholesky.133 = f32[128,128]{1,0:T(8,128)S(1)} custom-call(f32[128,128]{1,0:T(8,128)S(1)} %fusion.26), custom_call_target="Cholesky" | custom-call | tf_op jit(solution)/shard_map/jit(cholesky)/cholesky | solution.py:17
  735.6 9.8 %custom-call.23 = f32[1,128,128]{1,2,0:T(8,128)S(1)} custom-call(f32[1,128,128]{2,1,0:T(8,128)S(1)} %get-tuple-element.53), custom_call_target="InvertDiagBlocksLowerTriangular" | custom-call | tf_op jit(solution)/shard_map/triangular_solve/custom-call.0 | solution.py:18
  745.4 4.6 convert_select_fusion
  750.1 5.8 scatter.6
  755.9 40.0 %psum.55 = f32[5]{0:T(128)} all-reduce(f32[5]{0:T(128)S(1)} %fusion.61), channel_id=1, replica_groups=mesh['grp'=4,'mem'=8] {'grp','mem'}, use_global_device_ids=true, to_apply=%region_24.28 | all-reduce | flops 5 | bytes 40 | tf_op jit(solution)/shard_map/psum | solution.py:102
  798.0 30.0 %all-reduce.19.cloned.1.call-done = bf16[4096,128]{0,1:T(8,128)(2,1)} async-done(((bf16[4096,128]{0,1:T(8,128)(2,1)}), bf16[4096,128]{0,1:T(8,128)(2,1)}) %all-reduce.19.cloned.1.call-update) | async-done | bytes 1048592 | tf_op jit(solution)/shard_map/psum | solution.py:12
  (100 shorter events, 72.9 us)
Async XLA Ops:
  7.2 146.4 %all-reduce.9.cloned.1.call-start = ((), (), s32[]{:S(2)}) async-start(), calls=%async_computation | async-start | bytes 2097152 | tf_op jit(solution)/shard_map/psum | solution.py:12
  77.2 192.3 %all-reduce.11.cloned.1.call-start = ((), (), s32[]{:S(2)}) async-start(), calls=%async_computation.1 | async-start | bytes 2097152 | tf_op jit(solution)/shard_map/psum | solution.py:12
  191.8 193.9 %all-reduce.13.cloned.1.call-start = ((), (), s32[]{:S(2)}) async-start(), calls=%async_computation.2 | async-start | bytes 2097152 | tf_op jit(solution)/shard_map/psum | solution.py:12
  307.9 295.2 %all-reduce.15.cloned.1.call-start = ((), (), s32[]{:S(2)}) async-start(), calls=%async_computation.3 | async-start | bytes 16777216 | tf_op jit(solution)/shard_map/psum | solution.py:71
  450.6 260.2 %all-reduce.17.cloned.1.call-start = ((), (), s32[]{:S(2)}) async-start(), calls=%async_computation.4 | async-start | bytes 2097152 | tf_op jit(solution)/shard_map/psum | solution.py:12
  632.4 195.6 %all-reduce.19.cloned.1.call-start = ((), (), s32[]{:S(2)}) async-start(), calls=%async_computation.5 | async-start | bytes 2097152 | tf_op jit(solution)/shard_map/psum | solution.py:12
  715.9 3.2 copy-start
Sparse Core Ops, SparseCore 0:
  77.3 76.1 all-reduce.8
  191.9 77.5 all-reduce.10
  308.0 77.6 all-reduce.12
  450.7 152.4 all-reduce.14
  632.5 78.2 all-reduce.16
  750.2 77.7 all-reduce.18
where the time goes:
time: 851 us; the launch traced here: 842 us
  waiting for transfers between devices  466 us (55%)
  other arithmetic  153 us (18%)
  local copies, waits for them, and re-layouts  91.6 us (11%)
  blocking collectives  53 us (6%)
  matrix products  48.7 us (6%)
  between operations  28.3 us (3%)
    psum x5, waiting for transfers between devices, broadcast(): return lax.psum(jnp.where(mine, value, jnp.zeros_like(value)), axis)  327 us
    psum x1, waiting for transfers between devices, local(): lax.psum(placed.reshape(front_order, cols_local) + placed_front, 'grp')  138 us
    another operation x15, other arithmetic, factor_panel(): factor = jnp.linalg.cholesky(jnp.where(holder, diagonal_block, eye_block))  61.9 us
    another operation x10, other arithmetic, factor_panel(): lax.linalg.triangular_solve(factor, column, left_side=False, lower=True,...  52.3 us
    psum x1, blocking collectives, local(): log_det = lax.psum(terms, ('grp', 'mem'))  40 us
    reshape x2, local copies, waits for them, and re-layouts, local(): jnp.where(keep_cols[None, :, None], blocks, 0.0)  28.9 us
    dot_general x3, matrix products, local(): jnp.einsum('rc,jbc->rjb', shared, across, preferred_element_type=jnp.floa...  23.2 us
    another operation x5, matrix products, factor_panel(): lax.linalg.triangular_solve(factor, column, left_side=False, lower=True,...  18 us
  transfers between devices with their start and end apart: 6, of which 6 were waited for; matrix products, arithmetic and copies ran while one was open for 3% of the time, Pallas kernels for 0%

commit v1 on v0

--- a/solution.py
+++ b/solution.py
@@ -99,7 +99,7 @@
     terms = jnp.where(places == my_group, leaf_logs / (PL * block_width), 0.0) + jnp.where(
         places == groups, root_logs / (PR * block_width), 0.0
     )
-    log_det = lax.psum(terms, ("grp", "mem"))
+    log_det = lax.psum(lax.psum(terms, "mem"), "grp")
     return (root_factor, log_det)
 
 

time: 851 us -> 852 us (level)
  blocking collectives: 53 us -> 40 us
  waiting for transfers between devices: 466 us -> 479 us
    psum x1 -> x2, blocking collectives: 40 us -> 27 us  [local(): log_det = lax.psum(lax.psum(terms, 'mem'), 'grp')]
    psum x1, waiting for transfers between devices: 138 us -> 150 us  [local(): lax.psum(placed.reshape(front_order, cols_local) + placed_front, 'grp')]
    unnamed x10 -> x12, local copies, waits for them, and re-layouts: 17.4 us -> 17.4 us
where the time goes in v1:
time: 852 us; the launch traced here: 843 us
  waiting for transfers between devices  479 us (56%)
  other arithmetic  154 us (18%)
  local copies, waits for them, and re-layouts  91.6 us (11%)
  matrix products  49.4 us (6%)
  blocking collectives  40 us (5%)
  between operations  28.3 us (3%)
    psum x5, waiting for transfers between devices, broadcast(): return lax.psum(jnp.where(mine, value, jnp.zeros_like(value)), axis)  328 us
    psum x1, waiting for transfers between devices, local(): lax.psum(placed.reshape(front_order, cols_local) + placed_front, 'grp')  150 us
    another operation x15, other arithmetic, factor_panel(): factor = jnp.linalg.cholesky(jnp.where(holder, diagonal_block, eye_block))  61.9 us
    another operation x10, other arithmetic, factor_panel(): lax.linalg.triangular_solve(factor, column, left_side=False, lower=True,...  52.3 us
    reshape x2, local copies, waits for them, and re-layouts, local(): jnp.where(keep_cols[None, :, None], blocks, 0.0)  28.9 us
    psum x2, blocking collectives, local(): log_det = lax.psum(lax.psum(terms, 'mem'), 'grp')  27 us
    dot_general x3, matrix products, local(): jnp.einsum('rc,jbc->rjb', shared, across, preferred_element_type=jnp.floa...  23.2 us
    another operation x5, matrix products, factor_panel(): lax.linalg.triangular_solve(factor, column, left_side=False, lower=True,...  18.6 us
  transfers between devices with their start and end apart: 6, of which 6 were waited for; matrix products, arithmetic and copies ran while one was open for 3% of the time, Pallas kernels for 0%

profile of v1, /device:TPU:0, one launch (start us, length us, event | category | flops | bytes accessed | tf_op | source)
XLA Modules:
  0.0 843.3 jit_solution(11512504052918849375)
XLA Ops:
  9.9 13.1 %all-reduce.1 = s32[32]{0:T(128)S(1)} all-reduce(s32[32]{0:T(128)S(1)} %get-tuple-element.74), channel_id=1, replica_groups=mesh['grp'=4,'mem'=8] {'mem'}, use_global_device_ids=true, to_apply=%add.1 | all-reduce | flops 32 | bytes 256 | tf_op jit(solution)/shard_map/squeeze | solution.py:38
  27.6 8.9 %copy.38 = f32[1,4096,512]{1,2,0:T(8,128)} copy(f32[1,4096,512]{2,1,0:T(8,128)} %param.14) | data formatting | bytes 16777216 | tf_op args[0]
  36.6 8.9 %copy.44 = f32[4096,4,128]{2,0,1:T(8,128)} copy(f32[4096,4,128]{0,2,1:T(8,128)} %bitcast.141) | data formatting | bytes 16777216 | tf_op jit(solution)/shard_map/reshape;squeeze | solution.py:41
  51.4 11.7 %cholesky.89 = f32[128,128]{1,0:T(8,128)S(1)} custom-call(f32[128,128]{1,0:T(8,128)S(1)} %fusion.34), custom_call_target="Cholesky" | custom-call | tf_op jit(solution)/shard_map/jit(cholesky)/cholesky | solution.py:17
  64.4 9.8 %custom-call.19 = f32[1,128,128]{1,2,0:T(8,128)S(1)} custom-call(f32[1,128,128]{2,1,0:T(8,128)S(1)} %get-tuple-element.61), custom_call_target="InvertDiagBlocksLowerTriangular" | custom-call | tf_op jit(solution)/shard_map/triangular_solve/custom-call.0 | solution.py:18
  79.8 73.8 %all-reduce.9.cloned.1.call-done = bf16[4096,128]{0,1:T(8,128)(2,1)} async-done(((bf16[4096,128]{0,1:T(8,128)(2,1)}), bf16[4096,128]{0,1:T(8,128)(2,1)}) %all-reduce.9.cloned.1.call-update) | async-done | bytes 1048592 | tf_op jit(solution)/shard_map/psum | solution.py:12
  155.8 8.8 %select_reduce_fusion.1 = (f32[4096,128]{1,0:T(8,128)S(1)}, f32[4096,4,128]{2,0,1:T(8,128)}) fusion(pred[4]{0:T(512)(128)(4,1)S(1)} %get-tuple-element.71, f32[4096,4,128]{2,0,1:T(8,128)} %copy.44, bf16[4,128,128]{2,1,0:T(8,128)(2,1)S(1)} %gather_fusion.6, pred[4]{0:T(512)(128)(4,1)S(1)} %get-tuple-element.72, ...), kind=kOutput, calls=%fused_computation.12 | convolution fusion | flops 542703616 | bytes 20054024 | tf_op jit(solution)/shard_map/rc,jbc->rjb/dot_general | solution.py:57
  166.0 11.7 %cholesky.100 = f32[128,128]{1,0:T(8,128)S(1)} custom-call(f32[128,128]{1,0:T(8,128)S(1)} %fusion.32), custom_call_target="Cholesky" | custom-call | tf_op jit(solution)/shard_map/jit(cholesky)/cholesky | solution.py:17
  179.0 9.8 %custom-call.20 = f32[1,128,128]{1,2,0:T(8,128)S(1)} custom-call(f32[1,128,128]{2,1,0:T(8,128)S(1)} %get-tuple-element.59), custom_call_target="InvertDiagBlocksLowerTriangular" | custom-call | tf_op jit(solution)/shard_map/triangular_solve/custom-call.0 | solution.py:18
  194.8 74.7 %all-reduce.11.cloned.1.call-done = bf16[4096,128]{0,1:T(8,128)(2,1)} async-done(((bf16[4096,128]{0,1:T(8,128)(2,1)}), bf16[4096,128]{0,1:T(8,128)(2,1)}) %all-reduce.11.cloned.1.call-update) | async-done | bytes 1048592 | tf_op jit(solution)/shard_map/psum | solution.py:12
  271.7 8.8 %select_reduce_fusion = (f32[4096,128]{1,0:T(8,128)S(1)}, f32[4096,4,128]{2,0,1:T(8,128)}) fusion(pred[4]{0:T(512)(128)(4,1)S(1)} %get-tuple-element.69, f32[4096,4,128]{2,0,1:T(8,128)} %get-tuple-element.77, bf16[4,128,128]{2,1,0:T(8,128)(2,1)S(1)} %gather_fusion.7, pred[4]{0:T(512)(128)(4,1)S(1)} %get-tuple-element.72, ...), kind=kOutput, calls=%fused_computation.11 | convolution fusion | flops 542703616 | bytes 20054024 | tf_op jit(solution)/shard_map/rc,jbc->rjb/dot_general | solution.py:57
  282.1 11.7 %cholesky.111 = f32[128,128]{1,0:T(8,128)S(1)} custom-call(f32[128,128]{1,0:T(8,128)S(1)} %fusion.30), custom_call_target="Cholesky" | custom-call | tf_op jit(solution)/shard_map/jit(cholesky)/cholesky | solution.py:17
  295.1 9.8 %custom-call.21 = f32[1,128,128]{1,2,0:T(8,128)S(1)} custom-call(f32[1,128,128]{2,1,0:T(8,128)S(1)} %get-tuple-element.57), custom_call_target="InvertDiagBlocksLowerTriangular" | custom-call | tf_op jit(solution)/shard_map/triangular_solve/custom-call.0 | solution.py:18
  310.2 75.5 %all-reduce.13.cloned.1.call-done = bf16[4096,128]{0,1:T(8,128)(2,1)} async-done(((bf16[4096,128]{0,1:T(8,128)(2,1)}), bf16[4096,128]{0,1:T(8,128)(2,1)}) %all-reduce.13.cloned.1.call-update) | async-done | bytes 1048592 | tf_op jit(solution)/shard_map/psum | solution.py:12
  387.9 5.5 subtract_select_fusion
  393.5 18.6 %copy.73 = f32[4096,4,128]{2,1,0:T(4,128)} copy(f32[4096,4,128]{2,0,1:T(8,128)S(1)} %subtract_select_fusion) | data formatting | bytes 16777216 | tf_op jit(solution)/shard_map/reshape | solution.py:61
  412.1 10.3 %reshape.387 = f32[32,128,512]{2,1,0:T(8,128)} reshape(f32[4096,4,128]{2,1,0:T(4,128)} %copy.73) | data formatting | bytes 16777216 | tf_op jit(solution)/shard_map/reshape | solution.py:61
  422.4 7.7 gather_fusion
  430.1 8.9 %copy.74 = f32[4096,512]{0,1:T(8,128)} copy(f32[4096,512]{1,0:T(8,128)} %bitcast.140) | data formatting | bytes 16777216 | tf_op jit(solution)/shard_map/jit(_take)/gather | solution.py:69
  439.0 8.3 select_select_fusion
  452.7 150.4 %all-reduce.15.cloned.1.call-done = f32[4096,512]{0,1:T(8,128)} async-done(((f32[4096,512]{0,1:T(8,128)}), f32[4096,512]{0,1:T(8,128)}) %all-reduce.15.cloned.1.call-update) | async-done | bytes 8388624 | tf_op jit(solution)/shard_map/psum | solution.py:71
  605.0 11.7 %cholesky.122 = f32[128,128]{1,0:T(8,128)S(1)} custom-call(f32[128,128]{1,0:T(8,128)S(1)} %fusion.28), custom_call_target="Cholesky" | custom-call | tf_op jit(solution)/shard_map/jit(cholesky)/cholesky | solution.py:17
  618.0 9.8 %custom-call.22 = f32[1,128,128]{1,2,0:T(8,128)S(1)} custom-call(f32[1,128,128]{2,1,0:T(8,128)S(1)} %get-tuple-element.55), custom_call_target="InvertDiagBlocksLowerTriangular" | custom-call | tf_op jit(solution)/shard_map/triangular_solve/custom-call.0 | solution.py:18
  647.6 63.2 %all-reduce.17.cloned.1.call-done = bf16[4096,128]{0,1:T(8,128)(2,1)} async-done(((bf16[4096,128]{0,1:T(8,128)(2,1)}), bf16[4096,128]{0,1:T(8,128)(2,1)}) %all-reduce.17.cloned.1.call-update) | async-done | bytes 1048592 | tf_op jit(solution)/shard_map/psum | solution.py:12
  710.9 5.1 convolution_subtract_fusion
  720.1 11.7 %cholesky.133 = f32[128,128]{1,0:T(8,128)S(1)} custom-call(f32[128,128]{1,0:T(8,128)S(1)} %fusion.26), custom_call_target="Cholesky" | custom-call | tf_op jit(solution)/shard_map/jit(cholesky)/cholesky | solution.py:17
  735.7 9.8 %custom-call.23 = f32[1,128,128]{1,2,0:T(8,128)S(1)} custom-call(f32[1,128,128]{2,1,0:T(8,128)S(1)} %get-tuple-element.53), custom_call_target="InvertDiagBlocksLowerTriangular" | custom-call | tf_op jit(solution)/shard_map/triangular_solve/custom-call.0 | solution.py:18
  745.5 5.3 convert_select_fusion
  753.0 20.8 %psum.62 = f32[5]{0:T(128)S(1)} all-reduce(f32[5]{0:T(128)S(1)} %fusion.61), channel_id=1, replica_groups=mesh['grp'=4,'mem'=8] {'mem'}, use_global_device_ids=true, to_apply=%region_24.28 | all-reduce | flops 5 | bytes 40 | tf_op jit(solution)/shard_map/psum | solution.py:102
  773.8 5.8 scatter.6
  779.6 6.1 psum.63
  787.9 41.2 %all-reduce.19.cloned.1.call-done = bf16[4096,128]{0,1:T(8,128)(2,1)} async-done(((bf16[4096,128]{0,1:T(8,128)(2,1)}), bf16[4096,128]{0,1:T(8,128)(2,1)}) %all-reduce.19.cloned.1.call-update) | async-done | bytes 1048592 | tf_op jit(solution)/shard_map/psum | solution.py:12
  (103 shorter events, 77.6 us)
Async XLA Ops:
  7.2 146.4 %all-reduce.9.cloned.1.call-start = ((), (), s32[]{:S(2)}) async-start(), calls=%async_computation | async-start | bytes 2097152 | tf_op jit(solution)/shard_map/psum | solution.py:12
  77.2 192.3 %all-reduce.11.cloned.1.call-start = ((), (), s32[]{:S(2)}) async-start(), calls=%async_computation.1 | async-start | bytes 2097152 | tf_op jit(solution)/shard_map/psum | solution.py:12
  191.8 193.9 %all-reduce.13.cloned.1.call-start = ((), (), s32[]{:S(2)}) async-start(), calls=%async_computation.2 | async-start | bytes 2097152 | tf_op jit(solution)/shard_map/psum | solution.py:12
  307.9 295.2 %all-reduce.15.cloned.1.call-start = ((), (), s32[]{:S(2)}) async-start(), calls=%async_computation.3 | async-start | bytes 16777216 | tf_op jit(solution)/shard_map/psum | solution.py:71
  450.6 260.3 %all-reduce.17.cloned.1.call-start = ((), (), s32[]{:S(2)}) async-start(), calls=%async_computation.4 | async-start | bytes 2097152 | tf_op jit(solution)/shard_map/psum | solution.py:12
  632.4 196.6 %all-reduce.19.cloned.1.call-start = ((), (), s32[]{:S(2)}) async-start(), calls=%async_computation.5 | async-start | bytes 2097152 | tf_op jit(solution)/shard_map/psum | solution.py:12
  715.9 3.2 copy-start
  753.0 32.7 %copy-start.1 = (f32[4096,128]{0,1:T(8,128)S(1)}, f32[4096,128]{0,1:T(8,128)}, u32[]{:S(2)}) copy-start(f32[4096,128]{0,1:T(8,128)} %get-tuple-element.83) | copy-start | bytes 6291460
Sparse Core Ops, SparseCore 0:
  77.3 76.1 all-reduce.8
  191.9 77.5 all-reduce.10
  308.0 77.6 all-reduce.12
  450.7 152.4 all-reduce.14
  632.5 78.3 all-reduce.16
  750.9 78.0 all-reduce.18
